TPU v7x, 32 devices: a whole 2x2x4 slice. The times are simulated.
32 devices in a mesh: geom: 2 (over x), op: 8 (over z, y), col: 2 (over core).
Axes of the slice: x: 2, y: 2, z: 4, core: 2. Of those that a mesh axis runs over, the one named last changes fastest.
Arguments:
- wave_coef: float32 [2048, 1024], P('geom', 'col'), parts along dimension 0, may hold values from -6 to 6
- diag_energy: float32 [2048, 1024], P('geom', 'col'), parts along dimension 0, may hold values from -4 to 4
- left_block: bfloat16 [32, 1024, 1024], P(('geom', 'op')), parts along dimension 0, may hold values from -0.1875 to 0.1875
- right_block: bfloat16 [32, 1024, 1024], P(('geom', 'op'), None, 'col'), parts along dimension 0, may hold values from -0.1875 to 0.1875
- block_mask: int32 [32, 8, 8], P(('geom', 'op')), parts along dimension 0, may hold values 0 or 1
Outputs:
- new_wave: float32 [2048, 1024], P('geom', 'col'), parts along dimension 0
There are 2 independent parts, one for each index of `geom`. A program takes and returns all parts, laid end to end along the dimension named above; each array names one. Nothing has to cross between parts.
All inputs are finite; a program needn't handle non-finite values. No bound on the sum of `block_mask` on one device may be relied on, other than what follows from the above.
Results may differ from a plain program's by a relative error of at most 0.0042.
The roundings to bfloat16 on the way count: a program that leaves them out, or rounds other values in their place, can miss the bound.
Values may be sent and summed in bfloat16 or wider, within the bound.
A program may use at most 64 MiB of HBM per device.

v0:
```python
import jax
import jax.numpy as jnp
from jax import lax
from jax.sharding import PartitionSpec as P

M = 1024
STEPS = 2


def apply_mask(left_block, block_mask):
    total, width, _ = left_block.shape
    blocks = block_mask.shape[1]
    inside = width // blocks
    grid = left_block.reshape(total, blocks, inside, blocks, inside)
    keep = block_mask.astype(jnp.bfloat16)[:, :, None, :, None]
    return (grid * keep).reshape(total, width, width)


def correct(coef, sigma, diag_energy, correlation, weight, cells):
    theta = correlation / cells / (weight / cells + 1e-06)
    spacing = diag_energy - theta
    correction = (sigma - theta * coef) * spacing / jnp.maximum(spacing * spacing, 1.0)
    return coef - correction


def update_cols(coef, sigma, diag_energy, cells):
    correlation, weight = lax.psum((jnp.sum(coef * sigma), jnp.sum(coef * coef)), "col")
    moved = correct(coef, sigma, diag_energy, correlation, weight, cells)
    norm_sum = lax.psum(jnp.sum(moved * moved), "col")
    return moved * lax.rsqrt(norm_sum / cells + 1e-06)


def local(wave_coef, diag_energy, left_block, right_block, block_mask):
    masked = apply_mask(left_block, block_mask)
    cells = float(M * M)
    coef = wave_coef
    wave = wave_coef.astype(jnp.bfloat16)
    for step in range(STEPS):
        wave = coef.astype(jnp.bfloat16)
        inner = jnp.einsum(
            "mj,kjc->kmc",
            lax.all_gather(wave, "col", axis=1, tiled=True),
            right_block,
            preferred_element_type=jnp.float32,
        ).astype(jnp.bfloat16)
        partial_sum = jnp.einsum("kab,kbc->ac", masked, inner, preferred_element_type=jnp.float32)
        sigma = lax.psum(partial_sum, "op")
        coef = update_cols(coef, sigma, diag_energy, cells)
    return coef


def solution(mesh):
    in_specs = (
        P("geom", "col"),
        P("geom", "col"),
        P(("geom", "op"), None, None),
        P(("geom", "op"), None, "col"),
        P(("geom", "op"), None, None),
    )
    out_specs = P("geom", "col")
    return jax.shard_map(local, mesh=mesh, in_specs=in_specs, out_specs=out_specs, check_vma=False)
```

profile of v0, /device:TPU:0, one launch (start us, length us, event | category | flops | bytes accessed | tf_op | source)
XLA Modules:
  0.0 310.1 jit_solution(6017176165767036142)
XLA Ops:
  6.5 0.0 copy-start
  6.5 0.0 copy-start.1
  6.5 0.0 all-gather.3.cloned.1.call-start
  6.5 2.9 convert_element_type.22
  9.4 0.0 all-gather.3.cloned.1.call-update
  9.4 0.0 all-reduce.5.cloned.1.call-start
  9.5 0.0 copy-done.1
  9.5 2.5 mul.65
  12.0 7.4 %mul.66 = bf16[2,1024,1024]{2,1,0:T(8,128)(2,1)} reshape(bf16[2,8,128,8,128]{4,3,2,1,0:T(8,128)(2,1)} %mul.65) | data formatting | bytes 8388608 | tf_op jit(solution)/shard_map/mul | solution.py:16
  19.4 8.1 %mul.67 = bf16[2,1024,1024]{2,1,0:T(8,128)(2,1)} multiply(bf16[2,1024,1024]{2,1,0:T(8,128)(2,1)} %param.7, bf16[2,1024,1024]{2,1,0:T(8,128)(2,1)} %mul.66) | non-fusion elementwise | flops 2097152 | bytes 12582912 | tf_op jit(solution)/shard_map/mul | solution.py:16
  27.5 0.0 all-gather.3.cloned.1.call-done
  27.5 0.0 copy-done
  27.5 8.7 %fusion.10 = f32[1024,512]{1,0:T(8,128)} fusion(bf16[2,1024,1024]{2,1,0:T(8,128)(2,1)} %mul.67, bf16[2,1024,512]{2,1,0:T(8,128)(2,1)S(1)} %copy-done, bf16[1024,1024]{1,0:T(8,128)(2,1)} %all-gather.3.cloned.1.call-done), kind=kOutput, calls=%fused_computation.19 | convolution fusion | flops 4296015872 | bytes 10485760 | tf_op jit(solution)/shard_map/kab,kbc->ac/dot_general | solution.py:46
  36.1 0.0 all-reduce.5.cloned.1.call-update
  36.2 0.0 all-gather.5.cloned.1.call-start
  36.2 104.7 %all-reduce.5.cloned.1.call-done = f32[1024,512]{1,0:T(8,128)} async-done(((f32[1024,512]{1,0:T(8,128)}), f32[1024,512]{1,0:T(8,128)}) %all-reduce.5.cloned.1.call-update) | async-done | bytes 2097168 | tf_op jit(solution)/shard_map/psum | solution.py:47
  140.9 3.4 %multiply_reduce_fusion.4 = (f32[]{:T(128)}, f32[]{:T(128)}) fusion(f32[1024,512]{1,0:T(8,128)} %param.5, f32[1024,512]{1,0:T(8,128)} %all-reduce.5.cloned.1.call-done), kind=kLoop, calls=%fused_computation.15 | loop fusion | flops 2097150 | bytes 4194312 | tf_op jit(solution)/shard_map/reduce_sum | solution.py:27
  144.3 3.1 %all-reduce.1 = (f32[]{:T(128)}, f32[]{:T(128)}) all-reduce(f32[]{:T(128)} %get-tuple-element.8, f32[]{:T(128)} %get-tuple-element.7), channel_id=1, replica_groups=mesh['geom'=2,'op'=8,'col'=2] {'col'}, use_global_device_ids=true, to_apply=%region_2.0 | all-reduce | flops 2 | bytes 16 | tf_op jit(solution)/shard_map/psum | solution.py:27
  148.7 5.6 %multiply_reduce_fusion.3 = (f32[]{:T(128)}, f32[1024,512]{1,0:T(8,128)}) fusion(f32[1024,512]{1,0:T(8,128)} %param.5, f32[1024,512]{1,0:T(8,128)} %param.6, f32[1024,512]{1,0:T(8,128)} %all-reduce.5.cloned.1.call-done, f32[]{:T(128)S(6)} %div.32), kind=kLoop, calls=%fused_computation.13 | loop fusion | flops 5242879 | bytes 8388616 | tf_op jit(solution)/shard_map/reduce_sum | solution.py:29
  154.3 3.1 %psum.59 = f32[]{:T(128)} all-reduce(f32[]{:T(128)} %get-tuple-element.15), channel_id=1, replica_groups=mesh['geom'=2,'op'=8,'col'=2] {'col'}, use_global_device_ids=true, to_apply=%region_6.0 | all-reduce | flops 1 | bytes 8 | tf_op jit(solution)/shard_map/psum | solution.py:29
  158.1 2.8 multiply_convert_fusion
  160.9 0.0 all-gather.5.cloned.1.call-update
  160.9 0.0 all-reduce.7.cloned.1.call-start
  161.0 10.0 %all-gather.5.cloned.1.call-done = bf16[1024,1024]{1,0:T(8,128)(2,1)} async-done(((bf16[1024,512]{1,0:T(8,128)(2,1)}), bf16[1024,1024]{1,0:T(8,128)(2,1)}) %all-gather.5.cloned.1.call-update) | async-done | bytes 2097168 | tf_op jit(solution)/shard_map/all_gather | solution.py:42
  170.9 8.6 %fusion.13 = f32[1024,512]{1,0:T(8,128)} fusion(bf16[2,1024,1024]{2,1,0:T(8,128)(2,1)} %mul.67, bf16[2,1024,512]{2,1,0:T(8,128)(2,1)S(1)} %copy-done, bf16[1024,1024]{1,0:T(8,128)(2,1)} %all-gather.5.cloned.1.call-done), kind=kOutput, calls=%fused_computation.20 | convolution fusion | flops 4296015872 | bytes 10485760 | tf_op jit(solution)/shard_map/kab,kbc->ac/dot_general | solution.py:46
  179.6 0.0 all-reduce.7.cloned.1.call-update
  179.6 103.6 %all-reduce.7.cloned.1.call-done = f32[1024,512]{1,0:T(8,128)} async-done(((f32[1024,512]{1,0:T(8,128)}), f32[1024,512]{1,0:T(8,128)}) %all-reduce.7.cloned.1.call-update) | async-done | bytes 2097168 | tf_op jit(solution)/shard_map/psum | solution.py:47
  283.2 3.4 %multiply_reduce_fusion.1 = (f32[]{:T(128)}, f32[]{:T(128)}) fusion(f32[1024,512]{1,0:T(8,128)} %get-tuple-element.16, f32[]{:T(128)S(6)} %rsqrt.6, f32[1024,512]{1,0:T(8,128)} %all-reduce.7.cloned.1.call-done), kind=kLoop, calls=%fused_computation.10 | loop fusion | flops 2621438 | bytes 4194316 | tf_op jit(solution)/shard_map/reduce_sum | solution.py:27
  286.6 3.1 all-reduce
  290.9 5.6 %multiply_reduce_fusion = (f32[]{:T(128)}, f32[1024,512]{1,0:T(8,128)}) fusion(f32[1024,512]{1,0:T(8,128)} %param.6, f32[1024,512]{1,0:T(8,128)} %all-reduce.7.cloned.1.call-done, f32[]{:T(128)S(6)} %div.37, f32[1024,512]{1,0:T(8,128)} %get-tuple-element.16, f32[]{:T(128)S(6)} %rsqrt.6), kind=kLoop, calls=%fused_computation.8 | loop fusion | flops 5767167 | bytes 8388620 | tf_op jit(solution)/shard_map/reduce_sum | solution.py:29
  296.5 3.2 %psum.63 = f32[]{:T(128)} all-reduce(f32[]{:T(128)} %get-tuple-element.13), channel_id=1, replica_groups=mesh['geom'=2,'op'=8,'col'=2] {'col'}, use_global_device_ids=true, to_apply=%region_13.0 | all-reduce | flops 1 | bytes 8 | tf_op jit(solution)/shard_map/psum | solution.py:29
  300.4 3.1 %broadcast_multiply_fusion = f32[1024,512]{1,0:T(8,128)} fusion(f32[1024,512]{1,0:T(8,128)} %get-tuple-element.14, f32[]{:T(128)S(6)} %rsqrt.7), kind=kLoop, calls=%fused_computation.21 | loop fusion | flops 524288 | bytes 4194308 | tf_op jit(solution)/shard_map/mul | solution.py:30
  (1 shorter events, 0.0 us)
Async XLA Ops:
  6.5 20.9 %copy-start = (bf16[2,1024,512]{2,1,0:T(8,128)(2,1)S(1)}, bf16[2,1024,512]{2,1,0:T(8,128)(2,1)}, u32[]{:S(2)}) copy-start(bf16[2,1024,512]{2,1,0:T(8,128)(2,1)} %param.8) | copy-start | bytes 6291460
  6.5 2.9 copy-start.1
  6.5 20.9 %all-gather.3.cloned.1.call-start = ((), (), s32[]{:S(2)}) async-start(), calls=%async_computation | async-start | bytes 3145728 | tf_op jit(solution)/shard_map/all_gather | solution.py:42
  9.4 131.5 %all-reduce.5.cloned.1.call-start = ((), (), s32[]{:S(2)}) async-start(), calls=%async_computation.1 | async-start | bytes 4194304 | tf_op jit(solution)/shard_map/psum | solution.py:47
  36.2 134.8 %all-gather.5.cloned.1.call-start = ((), (), s32[]{:S(2)}) async-start(), calls=%async_computation.2 | async-start | bytes 3145728 | tf_op jit(solution)/shard_map/all_gather | solution.py:42
  160.9 122.3 %all-reduce.7.cloned.1.call-start = ((), (), s32[]{:S(2)}) async-start(), calls=%async_computation.3 | async-start | bytes 4194304 | tf_op jit(solution)/shard_map/psum | solution.py:47
Sparse Core Ops, SparseCore 0:
  9.5 13.2 all-gather.2
  36.3 104.5 all-reduce.4
  161.0 9.8 all-gather.4
  179.7 103.4 all-reduce.6
where the time goes:
time: 311 us; the launch traced here: 310 us
  waiting for transfers between devices  218 us (70%)
  other arithmetic  34.9 us (11%)
  matrix products  17.3 us (6%)
  between operations  17 us (5%)
  blocking collectives  12.5 us (4%)
  local copies, waits for them, and re-layouts  9.93 us (3%)
    psum x2, waiting for transfers between devices, local(): sigma = lax.psum(partial_sum, 'op')  208 us
    dot_general x2, matrix products, local(): jnp.einsum('kab,kbc->ac', masked, inner, preferred_element_type=jnp.float32)  17.3 us
    reduce_sum x2, other arithmetic, update_cols(): norm_sum = lax.psum(jnp.sum(moved * moved), 'col')  11.2 us
    all_gather x2, waiting for transfers between devices, local(): lax.all_gather(wave, 'col', axis=1, tiled=True)  9.96 us
    mul x2, local copies, waits for them, and re-layouts, apply_mask(): return (grid * keep).reshape(total, width, width)  9.92 us
    mul x1, other arithmetic, apply_mask(): return (grid * keep).reshape(total, width, width)  8.05 us
    reduce_sum x2, other arithmetic, update_cols(): jnp.sum(coef * coef)  6.78 us
    psum x2, blocking collectives, update_cols(): norm_sum = lax.psum(jnp.sum(moved * moved), 'col')  6.27 us
  transfers between devices with their start and end apart: 4, of which 3 were waited for; matrix products, arithmetic and copies ran while one was open for 6% of the time, Pallas kernels for 0%

commit v1 on v0

v1 whole, which is shorter than its diff:
```python
import functools

import jax
import jax.numpy as jnp
from jax import lax
from jax.experimental import pallas as pl
from jax.experimental.pallas import tpu as pltpu
from jax.sharding import PartitionSpec as P

STEPS = 2
MESH = pl.DeviceIdType.MESH
F32 = jnp.float32
BF16 = jnp.bfloat16


def fold(total):
    return sum(total[:, i:i + 128] for i in range(0, total.shape[1], 128))


def whole(total):
    return jnp.sum(jnp.sum(total, axis=1, keepdims=True), axis=0, keepdims=True)


def rows8(product):
    return product.reshape(product.shape[0] // 8, 8, product.shape[1]).sum(0)


def kernel(
    groups, cells, wave_parts, tile,
    coef_hbm, diag_hbm, left_hbm, right_hbm, mask_ref,
    out_ref, norm_ref,
    coef, diag, left, right, masked, inner, wave_own, wave_other,
    own, y_out, y_in, z_out, z_in, sig, scal_out, scal_in,
    load_sem, wave_sem, y_sem, z_sem, zg_sem, yg_sem, scal_sem,
):
    op, col = lax.axis_index("op"), lax.axis_index("col")
    a, h = op // 2, lax.rem(op, 2)
    mate = a * 2 + 1 - h
    other = 1 - col
    width, cols = coef.shape
    pairs = left.shape[0]
    rows = width // (2 * groups)
    blocks = mask_ref.shape[1]
    inside = width // blocks

    loads = [
        pltpu.make_async_copy(src, dst, load_sem.at[i])
        for i, (src, dst) in enumerate(
            ((coef_hbm, coef), (right_hbm, right), (left_hbm, left), (diag_hbm, diag))
        )
    ]
    for load in loads:
        load.start()

    barrier = pltpu.get_barrier_semaphore()
    peers = [{"col": other}, {"op": mate}]
    peers += [{"op": lax.rem(a + 1 + j, groups) * 2 + h} for j in range(groups - 1)]
    for peer in peers:
        pl.semaphore_signal(barrier, inc=1, device_id=peer, device_id_type=MESH)
    loads[0].wait()
    pl.semaphore_wait(barrier, len(peers))

    started = []

    def send(src, dst, sems, device_id):
        copy = pltpu.make_async_remote_copy(
            src_ref=src, dst_ref=dst, send_sem=sems[0], recv_sem=sems[1],
            device_id=device_id, device_id_type=MESH,
        )
        copy.start()
        started.append(copy)
        return copy

    def at(index):
        return pl.ds(pl.multiple_of(index * rows, rows), rows)

    def share(step, event, totals):
        for i, total in enumerate(totals):
            scal_out[step, event, i] = fold(total)
        copy = send(
            scal_out.at[step, event], scal_in.at[step, event],
            (scal_sem.at[0, step, event], scal_sem.at[1, step, event]), {"col": other},
        )
        copy.wait_recv()
        return [whole(scal_out[step, event, i] + scal_in[step, event, i]) for i in range(len(totals))]

    zero = jnp.zeros((8, cols), F32)
    scale = None
    for step in range(STEPS):
        part = width // wave_parts
        wave_copies = []
        for r in range(wave_parts):
            span = pl.ds(r * part, part)
            value = coef[span, :]
            if scale is not None:
                value = value * scale
                coef[span, :] = value
            wave_own[step, span, :] = value.astype(BF16)
            wave_copies.append(send(
                wave_own.at[step, span], wave_other.at[step, span],
                (wave_sem.at[0, step, r], wave_sem.at[1, step, r]), {"col": other},
            ))
        if step == 0:
            loads[1].wait()
        mine = pl.ds(pl.multiple_of(col * cols, cols), cols)
        theirs = pl.ds(pl.multiple_of(other * cols, cols), cols)
        for r in range(wave_parts):
            span = pl.ds(r * part, part)
            wave_copies[r].wait_recv()
            for k in range(pairs):
                value = jnp.dot(wave_own[step, span, :], right[k, mine, :], preferred_element_type=F32)
                value += jnp.dot(wave_other[step, span, :], right[k, theirs, :], preferred_element_type=F32)
                inner[pl.ds(k * width + r * part, part), :] = value.astype(BF16)
        if step == 0:
            loads[2].wait()

            def mask_rows(i, carry):
                span = pl.ds(pl.multiple_of(i * inside, inside), inside)
                for k in range(pairs):
                    for j in range(blocks):
                        keep = jnp.full((inside, inside), mask_ref[k, i, j].astype(F32)).astype(BF16)
                        masked[span, k * width + j * inside:k * width + (j + 1) * inside] = (
                            left[k, span, j * inside:(j + 1) * inside] * keep
                        )
                return carry

            lax.fori_loop(0, blocks, mask_rows, 0)

        to_mate = []
        for j in range(groups):
            target = lax.rem(a + 1 + j, groups)
            span = pl.ds(pl.multiple_of(target * 2 * rows, 2 * rows), 2 * rows)
            value = jnp.dot(masked[span, :], inner[...], preferred_element_type=F32)
            low, high = value[:rows], value[rows:]
            y_out[step, j] = jnp.where(h == 0, high, low).astype(BF16)
            to_mate.append(send(
                y_out.at[step, j], y_in.at[step, j],
                (y_sem.at[0, step, j], y_sem.at[1, step, j]), {"op": mate},
            ))
            own[j] = jnp.where(h == 0, low, high)

        if step == 0:
            loads[3].wait()

        def weigh(i, acc):
            value = coef[pl.ds(pl.multiple_of(i * tile, tile), tile), :]
            return acc + rows8(value * value)

        weight = lax.fori_loop(0, width // tile, weigh, zero)

        to_group = []
        for j in range(groups):
            to_mate[j].wait_recv()
            value = own[j] + y_in[step, j].astype(F32)
            if j < groups - 1:
                z_out[step, j] = value.astype(BF16)
                to_group.append(send(
                    z_out.at[step, j], z_in.at[step, j],
                    (z_sem.at[0, step, j], z_sem.at[1, step, j]),
                    {"op": lax.rem(a + 1 + j, groups) * 2 + h},
                ))
        for j in range(groups - 1):
            to_group[j].wait_recv()
            value = value + z_in[step, j].astype(F32)
        sig[step, at(op), :] = value.astype(BF16)

        to_mate = [send(
            sig.at[step, at(op)], sig.at[step, at(op)],
            (yg_sem.at[0, step, groups - 1], yg_sem.at[1, step, groups - 1]), {"op": mate},
        )]
        to_group = [
            send(
                sig.at[step, at(op)], sig.at[step, at(op)],
                (zg_sem.at[0, step, j], zg_sem.at[1, step, j]),
                {"op": lax.rem(a + 1 + j, groups) * 2 + h},
            )
            for j in range(groups - 1)
        ]

        def correlate(index, acc):
            return acc + rows8(coef[at(index), :] * sig[step, at(index), :].astype(F32))

        correlation = correlate(op, zero)
        for j in range(groups - 1):
            to_group[j].wait_recv()
            source = lax.rem(a + groups - 1 - j, groups)
            arrived = at(source * 2 + h)
            to_mate.append(send(
                sig.at[step, arrived], sig.at[step, arrived],
                (yg_sem.at[0, step, j], yg_sem.at[1, step, j]), {"op": mate},
            ))
            correlation = correlate(source * 2 + h, correlation)
        to_mate[0].wait_recv()
        correlation = correlate(mate, correlation)
        for j in range(groups - 1):
            to_mate[1 + j].wait_recv()
            source = lax.rem(a + groups - 1 - j, groups)
            correlation = correlate(source * 2 + 1 - h, correlation)

        total, weight = share(step, 0, [correlation, weight])
        theta = total / cells / (weight / cells + 1e-06)
        target_ref = coef if step < STEPS - 1 else out_ref

        def move(i, acc):
            span = pl.ds(pl.multiple_of(i * tile, tile), tile)
            value = coef[span, :]
            spacing = diag[span, :] - theta
            correction = (sig[step, span, :].astype(F32) - theta * value) * spacing / jnp.maximum(spacing * spacing, 1.0)
            moved = value - correction
            target_ref[span, :] = moved
            return acc + rows8(moved * moved)

        norm = lax.fori_loop(0, width // tile, move, zero)
        (norm,) = share(step, 1, [norm])
        scale = lax.rsqrt(norm / cells + 1e-06)

    norm_ref[...] = jnp.broadcast_to(scale, norm_ref.shape)
    for copy in started:
        copy.wait_send()


def local(groups, sides, wave_coef, diag_energy, left_block, right_block, block_mask):
    width, cols = wave_coef.shape
    pairs = left_block.shape[0]
    rows = width // (2 * groups)
    parts = 4
    dma = pltpu.SemaphoreType.DMA
    vmem = pltpu.VMEM
    moved, scale = pl.pallas_call(
        functools.partial(kernel, groups, float(width * cols * sides), parts, 32),
        out_shape=(
            jax.ShapeDtypeStruct((width, cols), F32),
            jax.ShapeDtypeStruct((8, 128), F32),
        ),
        in_specs=[pl.BlockSpec(memory_space=pl.ANY)] * 4 + [pl.BlockSpec(memory_space=pltpu.SMEM)],
        out_specs=(pl.BlockSpec(memory_space=vmem), pl.BlockSpec(memory_space=vmem)),
        scratch_shapes=[
            vmem((width, cols), F32),
            vmem((width, cols), F32),
            vmem(left_block.shape, BF16),
            vmem(right_block.shape, BF16),
            vmem((width, pairs * width), BF16),
            vmem((pairs * width, cols), BF16),
            vmem((STEPS, width, cols), BF16),
            vmem((STEPS, width, cols), BF16),
            vmem((groups, rows, cols), F32),
            vmem((STEPS, groups, rows, cols), BF16),
            vmem((STEPS, groups, rows, cols), BF16),
            vmem((STEPS, groups - 1, rows, cols), BF16),
            vmem((STEPS, groups - 1, rows, cols), BF16),
            vmem((STEPS, width, cols), BF16),
            vmem((STEPS, 2, 2, 8, 128), F32),
            vmem((STEPS, 2, 2, 8, 128), F32),
            dma((4,)),
            dma((2, STEPS, parts)),
            dma((2, STEPS, groups)),
            dma((2, STEPS, groups - 1)),
            dma((2, STEPS, groups - 1)),
            dma((2, STEPS, groups)),
            dma((2, STEPS, 2)),
        ],
        compiler_params=pltpu.CompilerParams(
            collective_id=0, has_side_effects=True, vmem_limit_bytes=60 * 1024 * 1024
        ),
    )(wave_coef, diag_energy, left_block, right_block, block_mask)
    return moved * scale[0, 0]


def solution(mesh):
    in_specs = (
        P("geom", "col"),
        P("geom", "col"),
        P(("geom", "op"), None, None),
        P(("geom", "op"), None, "col"),
        P(("geom", "op"), None, None),
    )
    return jax.shard_map(
        functools.partial(local, mesh.shape["op"] // 2, mesh.shape["col"]),
        mesh=mesh, in_specs=in_specs, out_specs=P("geom", "col"), check_vma=False,
    )
```

time: 311 us -> 106 us (0.34)
  the two profiles are of different devices: /device:TPU:0 before, /device:TPU:19 now
where the time goes in v1:
time: 106 us
  Pallas kernels  101 us (95%)
  other arithmetic  3.75 us (4%)
  local copies, waits for them, and re-layouts  1.19 us (1%)
    pallas_call x1, Pallas kernels, local(): pl.pallas_call(functools.partial(kernel, groups, float(width * cols * sid...  101 us
    mul x1, other arithmetic, local(): return moved * scale[0, 0]  3.75 us

profile of v1, /device:TPU:19, one launch (start us, length us, event | category | flops | bytes accessed | tf_op | source)
XLA Modules:
  0.0 106.0 jit_solution(2538755539760331252)
XLA Ops:
  0.0 101.1 %shard_map.55 = (f32[1024,512]{1,0:T(8,128)}, f32[8,128]{1,0:T(8,128)}) custom-call(f32[1024,512]{1,0:T(8,128)} %coef_hbm.1, f32[1024,512]{1,0:T(8,128)} %diag_hbm.1, bf16[2,1024,1024]{2,1,0:T(8,128)(2,1)} %left_hbm.1, bf16[2,1024,512]{2,1,0:T(8,128)(2,1)} %right_hbm.1, s32[2,8,8]{2,1,0:T(8,128)} %mask_ref.1), custom_call_target="tpu_custom_call" | custom-call | tf_op jit(solution)/shard_map/pallas_call | solution.py:229
  101.1 1.2 %slice.3 = f32[1,1]{1,0:T(1,128)} slice(f32[8,128]{1,0:T(8,128)} %get-tuple-element.8), slice={[0:1], [0:1]} | slice | bytes 8 | tf_op jit(solution)/shard_map/slice | solution.py:266
  102.3 3.7 %broadcast_multiply_fusion = f32[1024,512]{1,0:T(8,128)} fusion(f32[1024,512]{1,0:T(8,128)} %get-tuple-element.7, f32[]{:T(128)} %bitcast), kind=kLoop, calls=%fused_computation | loop fusion | flops 524288 | bytes 4194308 | tf_op jit(solution)/shard_map/mul | solution.py:266

commit v2 on v1

v2 whole, which is shorter than its diff:
```python
import functools

import jax
import jax.numpy as jnp
from jax import lax
from jax.experimental import pallas as pl
from jax.experimental.pallas import tpu as pltpu
from jax.sharding import PartitionSpec as P

STEPS = 2
MESH = pl.DeviceIdType.MESH
F32 = jnp.float32
BF16 = jnp.bfloat16


def fold(total):
    return sum(total[:, i:i + 128] for i in range(0, total.shape[1], 128))


def whole(total):
    return jnp.sum(jnp.sum(total, axis=1, keepdims=True), axis=0, keepdims=True)


def rows8(product):
    return product.reshape(product.shape[0] // 8, 8, product.shape[1]).sum(0)


def kernel(
    groups, cells, wave_parts, tile,
    coef_hbm, diag_hbm, left_hbm, right_hbm, mask_ref,
    out_ref, norm_ref,
    coef, diag, left, right, masked, inner, wave_own, wave_other,
    own, y_out, y_in, z_out, z_in, sig, scal_out, scal_in,
    load_sem, wave_sem, y_sem, z_sem, zg_sem, yg_sem, scal_sem,
):
    op, col = lax.axis_index("op"), lax.axis_index("col")
    a, h = op // 2, lax.rem(op, 2)
    mate = a * 2 + 1 - h
    other = 1 - col
    width, cols = coef.shape
    pairs = left.shape[0]
    rows = width // (2 * groups)
    bands, band = inner.shape[0], inner.shape[2]
    blocks = mask_ref.shape[1]
    inside = width // blocks

    loads = [
        pltpu.make_async_copy(src, dst, load_sem.at[i])
        for i, (src, dst) in enumerate(
            ((coef_hbm, coef), (right_hbm, right), (left_hbm, left), (diag_hbm, diag))
        )
    ]
    for load in loads[:2]:
        load.start()

    barrier = pltpu.get_barrier_semaphore()
    peers = [{"col": other}, {"op": mate}]
    peers += [{"op": lax.rem(a + 1 + j, groups) * 2 + h} for j in range(groups - 1)]
    for peer in peers:
        pl.semaphore_signal(barrier, inc=1, device_id=peer, device_id_type=MESH)
    loads[0].wait()
    for load in loads[2:]:
        load.start()
    pl.semaphore_wait(barrier, len(peers))

    started = []

    def send(src, dst, sems, device_id):
        copy = pltpu.make_async_remote_copy(
            src_ref=src, dst_ref=dst, send_sem=sems[0], recv_sem=sems[1],
            device_id=device_id, device_id_type=MESH,
        )
        copy.start()
        started.append(copy)
        return copy

    def at(index):
        return pl.ds(pl.multiple_of(index * rows, rows), rows)

    def share(step, event, totals):
        for i, total in enumerate(totals):
            scal_out[step, event, i] = fold(total)
        copy = send(
            scal_out.at[step, event], scal_in.at[step, event],
            (scal_sem.at[0, step, event], scal_sem.at[1, step, event]), {"col": other},
        )
        copy.wait_recv()
        return [whole(scal_out[step, event, i] + scal_in[step, event, i]) for i in range(len(totals))]

    hops = (groups // 2, groups - 1 - groups // 2)
    legs = [(way, t) for t in range(hops[0]) for way in range(2) if t < hops[way]]

    def origin(way, t):
        return lax.rem(a + (groups - 1 - t if way == 0 else 1 + t), groups)

    zero = jnp.zeros((8, cols), F32)
    scale = None
    for step in range(STEPS):
        part = width // wave_parts
        wave_copies = []
        for r in range(wave_parts):
            span = pl.ds(r * part, part)
            value = coef[span, :]
            if scale is not None:
                value = value * scale
                coef[span, :] = value
            wave_own[step, span, :] = value.astype(BF16)
            wave_copies.append(send(
                wave_own.at[step, span], wave_other.at[step, span],
                (wave_sem.at[0, step, r], wave_sem.at[1, step, r]), {"col": other},
            ))
        if step == 0:
            loads[1].wait()
        mine = pl.ds(pl.multiple_of(col * cols, cols), cols)
        theirs = pl.ds(pl.multiple_of(other * cols, cols), cols)
        state = {"corr": jnp.zeros((8, band), F32)}
        mate_in, group_in, mate_back, group_back = {}, {}, {}, {}

        def contract(b):
            lanes = slice(b * band, (b + 1) * band)
            for r in range(wave_parts):
                span = pl.ds(r * part, part)
                if b == 0:
                    wave_copies[r].wait_recv()
                for k in range(pairs):
                    value = jnp.dot(wave_own[step, span, :], right[k, mine, lanes], preferred_element_type=F32)
                    value += jnp.dot(wave_other[step, span, :], right[k, theirs, lanes], preferred_element_type=F32)
                    inner[b, pl.ds(k * width + r * part, part), :] = value.astype(BF16)

        def apply_mask():
            loads[2].wait()

            def mask_rows(i, carry):
                span = pl.ds(pl.multiple_of(i * inside, inside), inside)
                for k in range(pairs):
                    for j in range(blocks):
                        keep = jnp.full((inside, inside), mask_ref[k, i, j].astype(F32)).astype(BF16)
                        masked[span, k * width + j * inside:k * width + (j + 1) * inside] = (
                            left[k, span, j * inside:(j + 1) * inside] * keep
                        )
                return carry

            lax.fori_loop(0, blocks, mask_rows, 0)

        def halves(b):
            mate_in[b] = []
            for j in range(groups):
                target = lax.rem(a + 1 + j, groups)
                span = pl.ds(pl.multiple_of(target * 2 * rows, 2 * rows), 2 * rows)
                value = jnp.dot(masked[span, :], inner[b], preferred_element_type=F32)
                low, high = value[:rows], value[rows:]
                y_out[step, b, j] = jnp.where(h == 0, high, low).astype(BF16)
                mate_in[b].append(send(
                    y_out.at[step, b, j], y_in.at[step, b, j],
                    (y_sem.at[0, step, b, j], y_sem.at[1, step, b, j]), {"op": mate},
                ))
                own[b, j] = jnp.where(h == 0, low, high)

        def to_owner(b):
            group_in[b] = []
            for j in range(groups):
                mate_in[b][j].wait_recv()
                value = own[b, j] + y_in[step, b, j].astype(F32)
                if j < groups - 1:
                    z_out[step, b, j] = value.astype(BF16)
                    group_in[b].append(send(
                        z_out.at[step, b, j], z_in.at[step, b, j],
                        (z_sem.at[0, step, b, j], z_sem.at[1, step, b, j]),
                        {"op": lax.rem(a + 1 + j, groups) * 2 + h},
                    ))
                else:
                    own[b, j] = value

        def correlate(b, index):
            lanes = slice(b * band, (b + 1) * band)
            state["corr"] += rows8(coef[at(index), lanes] * sig[step, b, at(index), :].astype(F32))

        def relay(b, way, t, source):
            chunk = sig.at[step, b, at(source)]
            slot = way * hops[0] + t
            group_back[b, way, t] = send(
                chunk, chunk, (zg_sem.at[0, step, b, slot], zg_sem.at[1, step, b, slot]),
                {"op": lax.rem(a + (1 if way == 0 else groups - 1), groups) * 2 + h},
            )

        def finish(b):
            value = own[b, groups - 1]
            for j in range(groups - 1):
                group_in[b][j].wait_recv()
                value = value + z_in[step, b, j].astype(F32)
            sig[step, b, at(op), :] = value.astype(BF16)
            chunk = sig.at[step, b, at(op)]
            for way, length in enumerate(hops):
                if length:
                    relay(b, way, 0, op)
            mate_back[b] = [send(
                chunk, chunk,
                (yg_sem.at[0, step, b, groups - 1], yg_sem.at[1, step, b, groups - 1]), {"op": mate},
            )]
            correlate(b, op)

        def forward(b):
            for way, t in legs:
                group_back[b, way, t].wait_recv()
                source = origin(way, t) * 2 + h
                if t + 1 < hops[way]:
                    relay(b, way, t + 1, source)
                chunk = sig.at[step, b, at(source)]
                slot = way * hops[0] + t
                mate_back[b].append(send(
                    chunk, chunk, (yg_sem.at[0, step, b, slot], yg_sem.at[1, step, b, slot]), {"op": mate},
                ))
                correlate(b, source)

        def collect(b):
            mate_back[b][0].wait_recv()
            correlate(b, mate)
            for i, (way, t) in enumerate(legs):
                mate_back[b][1 + i].wait_recv()
                correlate(b, origin(way, t) * 2 + 1 - h)

        for b in range(bands):
            contract(b)
            if step == 0 and b == 0:
                apply_mask()
            halves(b)
        if step == 0:
            loads[3].wait()

        def weigh(i, acc):
            value = coef[pl.ds(pl.multiple_of(i * tile, tile), tile), :]
            return acc + rows8(value * value)

        weight = lax.fori_loop(0, width // tile, weigh, zero)
        for b in range(bands):
            to_owner(b)
            if b > 0:
                forward(b - 1)
            finish(b)
            if b > 0:
                collect(b - 1)
        forward(bands - 1)
        collect(bands - 1)
        correlation = state["corr"]

        total, weight = share(step, 0, [correlation, weight])
        theta = total / cells / (weight / cells + 1e-06)
        target_ref = coef if step < STEPS - 1 else out_ref

        def move(i, acc):
            span = pl.ds(pl.multiple_of(i * tile, tile), tile)
            value = coef[span, :]
            spacing = diag[span, :] - theta
            sigma = jnp.concatenate([sig[step, b, span, :] for b in range(bands)], axis=1).astype(F32)
            correction = (sigma - theta * value) * spacing * pl.reciprocal(jnp.maximum(spacing * spacing, 1.0))
            moved = value - correction
            target_ref[span, :] = moved
            return acc + rows8(moved * moved)

        norm = lax.fori_loop(0, width // tile, move, zero)
        (norm,) = share(step, 1, [norm])
        scale = lax.rsqrt(norm / cells + 1e-06)

    norm_ref[...] = jnp.broadcast_to(scale, norm_ref.shape)
    for copy in started:
        copy.wait_send()


def local(groups, sides, wave_coef, diag_energy, left_block, right_block, block_mask):
    width, cols = wave_coef.shape
    pairs = left_block.shape[0]
    rows = width // (2 * groups)
    parts = 4
    bands = max(1, cols // 256)
    band = cols // bands
    dma = pltpu.SemaphoreType.DMA
    vmem = pltpu.VMEM
    moved, scale = pl.pallas_call(
        functools.partial(kernel, groups, float(width * cols * sides), parts, 32),
        out_shape=(
            jax.ShapeDtypeStruct((width, cols), F32),
            jax.ShapeDtypeStruct((8, cols), F32),
        ),
        in_specs=[pl.BlockSpec(memory_space=pl.ANY)] * 4 + [pl.BlockSpec(memory_space=pltpu.SMEM)],
        out_specs=(pl.BlockSpec(memory_space=vmem), pl.BlockSpec(memory_space=vmem)),
        scratch_shapes=[
            vmem((width, cols), F32),
            vmem((width, cols), F32),
            vmem(left_block.shape, BF16),
            vmem(right_block.shape, BF16),
            vmem((width, pairs * width), BF16),
            vmem((bands, pairs * width, band), BF16),
            vmem((STEPS, width, cols), BF16),
            vmem((STEPS, width, cols), BF16),
            vmem((bands, groups, rows, band), F32),
            vmem((STEPS, bands, groups, rows, band), BF16),
            vmem((STEPS, bands, groups, rows, band), BF16),
            vmem((STEPS, bands, groups - 1, rows, band), BF16),
            vmem((STEPS, bands, groups - 1, rows, band), BF16),
            vmem((STEPS, bands, width, band), BF16),
            vmem((STEPS, 2, 2, 8, 128), F32),
            vmem((STEPS, 2, 2, 8, 128), F32),
            dma((4,)),
            dma((2, STEPS, parts)),
            dma((2, STEPS, bands, groups)),
            dma((2, STEPS, bands, groups - 1)),
            dma((2, STEPS, bands, groups - 1)),
            dma((2, STEPS, bands, groups)),
            dma((2, STEPS, 2)),
        ],
        compiler_params=pltpu.CompilerParams(
            collective_id=0, has_side_effects=True, vmem_limit_bytes=60 * 1024 * 1024
        ),
    )(wave_coef, diag_energy, left_block, right_block, block_mask)
    return (moved.reshape(width // 8, 8, cols) * scale).reshape(width, cols)


def solution(mesh):
    in_specs = (
        P("geom", "col"),
        P("geom", "col"),
        P(("geom", "op"), None, None),
        P(("geom", "op"), None, "col"),
        P(("geom", "op"), None, None),
    )
    return jax.shard_map(
        functools.partial(local, mesh.shape["op"] // 2, mesh.shape["col"]),
        mesh=mesh, in_specs=in_specs, out_specs=P("geom", "col"), check_vma=False,
    )
```

time: 106 us -> 98.7 us (0.931)
  the two profiles are of different devices: /device:TPU:19 before, /device:TPU:0 now
where the time goes in v2:
time: 98.7 us; the launch traced here: 98.5 us
  Pallas kernels  95.3 us (97%)
  other arithmetic  3.14 us (3%)
    pallas_call x1, Pallas kernels, local(): pl.pallas_call(functools.partial(kernel, groups, float(width * cols * sid...  95.3 us
    mul x1, other arithmetic, local(): return (moved.reshape(width // 8, 8, cols) * scale).reshape(width, cols)  3.14 us

profile of v2, /device:TPU:0, one launch (start us, length us, event | category | flops | bytes accessed | tf_op | source)
XLA Modules:
  0.0 98.5 jit_solution(10970129023841644264)
XLA Ops:
  0.0 95.3 %shard_map.55 = (f32[1024,512]{1,0:T(8,128)}, f32[8,512]{1,0:T(8,128)}) custom-call(f32[1024,512]{1,0:T(8,128)} %coef_hbm.1, f32[1024,512]{1,0:T(8,128)} %diag_hbm.1, bf16[2,1024,1024]{2,1,0:T(8,128)(2,1)} %left_hbm.1, bf16[2,1024,512]{2,1,0:T(8,128)(2,1)} %right_hbm.1, s32[2,8,8]{2,1,0:T(8,128)} %mask_ref.1), custom_call_target="tpu_custom_call" | custom-call | tf_op jit(solution)/shard_map/pallas_call | solution.py:278
  95.3 3.1 %bitcast_multiply_fusion = f32[1024,512]{1,0:T(8,128)} fusion(f32[1024,512]{1,0:T(8,128)} %get-tuple-element.7, f32[8,512]{1,0:T(8,128)} %get-tuple-element.8), kind=kLoop, calls=%fused_computation | loop fusion | flops 524288 | bytes 4210688 | tf_op jit(solution)/shard_map/mul | solution.py:315

commit v3 on v2

--- a/solution.py
+++ b/solution.py
@@ -92,6 +92,11 @@
 
     def origin(way, t):
         return lax.rem(a + (groups - 1 - t if way == 0 else 1 + t), groups)
+
+    ahead = sorted(range(1, groups), key=lambda d: -min(d, groups - d)) + [groups]
+
+    def target_of(j):
+        return lax.rem(a + ahead[j], groups)
 
     zero = jnp.zeros((8, cols), F32)
     scale = None
@@ -145,7 +150,7 @@
         def halves(b):
             mate_in[b] = []
             for j in range(groups):
-                target = lax.rem(a + 1 + j, groups)
+                target = target_of(j)
                 span = pl.ds(pl.multiple_of(target * 2 * rows, 2 * rows), 2 * rows)
                 value = jnp.dot(masked[span, :], inner[b], preferred_element_type=F32)
                 low, high = value[:rows], value[rows:]
@@ -166,7 +171,7 @@
                     group_in[b].append(send(
                         z_out.at[step, b, j], z_in.at[step, b, j],
                         (z_sem.at[0, step, b, j], z_sem.at[1, step, b, j]),
-                        {"op": lax.rem(a + 1 + j, groups) * 2 + h},
+                        {"op": target_of(j) * 2 + h},
                     ))
                 else:
                     own[b, j] = value

time: 98.7 us -> 97.4 us (0.987)
  Pallas kernels: 95.3 us -> 94.1 us
    pallas_call x1, Pallas kernels: 95.3 us -> 94.1 us  [local(): pl.pallas_call(functools.partial(kernel, groups, float(width * cols * sid...]
where the time goes in v3:
time: 97.4 us; the launch traced here: 97.2 us
  Pallas kernels  94.1 us (97%)
  other arithmetic  3.14 us (3%)
    pallas_call x1, Pallas kernels, local(): pl.pallas_call(functools.partial(kernel, groups, float(width * cols * sid...  94.1 us
    mul x1, other arithmetic, local(): return (moved.reshape(width // 8, 8, cols) * scale).reshape(width, cols)  3.14 us

profile of v3, /device:TPU:0, one launch (start us, length us, event | category | flops | bytes accessed | tf_op | source)
XLA Modules:
  0.0 97.2 jit_solution(13389592250402231312)
XLA Ops:
  0.0 94.1 %shard_map.55 = (f32[1024,512]{1,0:T(8,128)}, f32[8,512]{1,0:T(8,128)}) custom-call(f32[1024,512]{1,0:T(8,128)} %coef_hbm.1, f32[1024,512]{1,0:T(8,128)} %diag_hbm.1, bf16[2,1024,1024]{2,1,0:T(8,128)(2,1)} %left_hbm.1, bf16[2,1024,512]{2,1,0:T(8,128)(2,1)} %right_hbm.1, s32[2,8,8]{2,1,0:T(8,128)} %mask_ref.1), custom_call_target="tpu_custom_call" | custom-call | tf_op jit(solution)/shard_map/pallas_call | solution.py:283
  94.1 3.1 %bitcast_multiply_fusion = f32[1024,512]{1,0:T(8,128)} fusion(f32[1024,512]{1,0:T(8,128)} %get-tuple-element.7, f32[8,512]{1,0:T(8,128)} %get-tuple-element.8), kind=kLoop, calls=%fused_computation | loop fusion | flops 524288 | bytes 4210688 | tf_op jit(solution)/shard_map/mul | solution.py:320
